TPU v7x, 32 devices: a whole 2x2x4 slice. The times are simulated.
32 devices in a mesh: ctx: 4 (over y, x), exp: 8 (over z, core).
Axes of the slice: x: 2, y: 2, z: 4, core: 2. Of those that a mesh axis runs over, the one named last changes fastest.
Arguments:
- inputs: bfloat16 [4, 6144, 768], P('ctx', 'exp'), may hold values from -6 to 6
- prev_logits: float32 [4, 6144, 12], P('ctx', 'exp'), may hold values from -4 to 4
- routes: int32 [4, 6144, 2], P('ctx', 'exp'), may hold values from 0 to 11, all different within a row; in each aligned block of 768 rows (0 to 767, 768 to 1535, ..., all dimensions but the last counted through in order) at most 144 rows name the same one
- attn_gain: float32 [768], replicated, may hold values from 0.25 to 1.75
- w_qkv: bfloat16 [768, 2304], replicated, may hold values from -0.21875 to 0.21875
- w_out: bfloat16 [768, 768], replicated, may hold values from -0.875 to 0.875
- moe_gain: float32 [768], replicated, may hold values from 0.25 to 1.75
- router: bfloat16 [768, 12], replicated, may hold values from -0.109375 to 0.109375
- const_gate: bfloat16 [2, 768, 2], replicated, may hold values from -0.21875 to 0.21875
- const_vec: float32 [2, 768], replicated, may hold values from -12 to 12
- w_gate: bfloat16 [8, 768, 2048], P('exp'), may hold values from -0.21875 to 0.21875
- w_up: bfloat16 [8, 768, 2048], P('exp'), may hold values from -0.21875 to 0.21875
- w_down: bfloat16 [8, 2048, 768], P('exp'), may hold values from -1.5 to 1.5
- out_grad: bfloat16 [4, 6144, 768], P('ctx', 'exp'), may hold values from -6 to 6
Outputs:
- mixed_out: bfloat16 [4, 6144, 768], P('ctx', 'exp')
- d_inputs: float32 [4, 6144, 768], P('ctx', 'exp')
- d_prev: float32 [4, 6144, 12], P('ctx', 'exp')
- d_attn_gain: float32 [768], replicated
- d_w_qkv: float32 [768, 2304], replicated
- d_w_out: float32 [768, 768], replicated
- d_moe_gain: float32 [768], replicated
- d_router: float32 [768, 12], replicated
- d_const_gate: float32 [2, 768, 2], replicated
- d_const_vec: float32 [2, 768], replicated
- d_w_gate: float32 [8, 768, 2048], P('exp', 'ctx')
- d_w_up: float32 [8, 768, 2048], P('exp', 'ctx')
- d_w_down: float32 [8, 2048, 768], P('exp', 'ctx')
Inputs may be any that keep to these rules, and one draw needn't show every extreme that they name: `routes`: each row names two different experts. Among the 768 rows of one device no expert is named by more than 144 rows, and on some devices one is named by exactly 144.
All inputs are finite; a program needn't handle non-finite values.
Results may differ from a plain program's by a relative error of at most 0.015.
Values may be sent and summed in bfloat16 or wider, within the bound.
No kernel may reach another device: no remote copies, remote signals or barrier semaphores. Data moves between devices by JAX's collectives and lax.ppermute only.
A program may use at most 256 MiB of HBM per device.

v0:
```python
from functools import partial
import jax
import jax.numpy as jnp
from jax import lax
from jax.sharding import PartitionSpec as P

HEADS = 12
HEAD_DIM = 64
FFN_EXPERTS = 8
ALL_EXPERTS = 12
CONT_LEN = 512
masked_value = -1e30
epsilon = 1e-06
highest = lax.Precision.HIGHEST


def rms_forward(tensor, gain_vec):
    inverse = lax.rsqrt(jnp.mean(tensor * tensor, axis=-1, keepdims=True) + epsilon)
    return (tensor * inverse * gain_vec, inverse)


def rms_backward(tensor, inverse, gain_vec, upstream):
    scaled = upstream * gain_vec
    d_gain = jnp.sum(upstream * tensor * inverse, axis=0)
    d_tensor = inverse * scaled - tensor * inverse**3 * jnp.mean(
        scaled * tensor, axis=-1, keepdims=True
    )
    return (d_tensor, d_gain)


def route_slots(route_rows):
    flat_ids = route_rows.reshape(-1)
    onehot = (flat_ids[:, None] == jnp.arange(ALL_EXPERTS, dtype=jnp.int32)[None, :]).astype(
        jnp.int32
    )
    before = jnp.cumsum(onehot, axis=0) - onehot
    return jnp.sum(before * onehot, axis=1).reshape(route_rows.shape)


def split_heads(tensor):
    reshaped = tensor.reshape(tensor.shape[:-1] + (HEADS, HEAD_DIM))
    return jnp.moveaxis(reshaped, -2, 0)


def join_heads(tensor):
    moved_axes = jnp.moveaxis(tensor, 0, -2)
    return moved_axes.reshape(moved_axes.shape[:-2] + (HEADS * HEAD_DIM,))


def head_forward(allowed, operands):
    queries, key_rows, value_rows = operands
    raw_scores = jnp.einsum(
        "qd,kd->qk", queries, key_rows, preferred_element_type=jnp.float32
    ) * HEAD_DIM ** (-0.5)
    masked = jnp.where(allowed, raw_scores, masked_value)
    row_peak = jnp.max(masked, axis=-1, keepdims=True)
    unnormed = jnp.exp(masked - row_peak)
    row_total = jnp.sum(unnormed, axis=-1, keepdims=True)
    weights_soft = (unnormed / row_total).astype(jnp.bfloat16)
    result = jnp.einsum("qk,kd->qd", weights_soft, value_rows, preferred_element_type=jnp.float32)
    return (result, row_peak[..., 0] + jnp.log(row_total[..., 0]))


def head_backward(allowed, operands):
    queries, key_rows, value_rows, upstream, log_total = operands
    raw_scores = jnp.einsum(
        "qd,kd->qk", queries, key_rows, preferred_element_type=jnp.float32
    ) * HEAD_DIM ** (-0.5)
    masked = jnp.where(allowed, raw_scores, masked_value)
    probs_full = jnp.where(allowed, jnp.exp(masked - log_total[..., None]), 0.0)
    d_values = jnp.einsum(
        "qk,qd->kd", probs_full.astype(jnp.bfloat16), upstream, preferred_element_type=jnp.float32
    )
    d_probs = jnp.einsum("qd,kd->qk", upstream, value_rows, preferred_element_type=jnp.float32)
    d_scores = probs_full * (d_probs - jnp.sum(probs_full * d_probs, axis=-1, keepdims=True))
    d_scores = d_scores.astype(jnp.bfloat16)
    d_queries = jnp.einsum(
        "qk,kd->qd", d_scores, key_rows, preferred_element_type=jnp.float32
    ) * HEAD_DIM ** (-0.5)
    d_keys = jnp.einsum(
        "qk,qd->kd", d_scores, queries, preferred_element_type=jnp.float32
    ) * HEAD_DIM ** (-0.5)
    return (d_queries, d_keys, d_values)


def body(
    inputs,
    prev_logits,
    routes,
    attn_gain,
    w_qkv,
    w_out,
    moe_gain,
    router,
    const_gate,
    const_vec,
    w_gate,
    w_up,
    w_down,
    out_grad,
):
    model_width = inputs.shape[2]
    tok_rows = inputs.shape[1]
    prompt_local = tok_rows - CONT_LEN
    prompt_len = prompt_local * lax.axis_size("ctx")
    split_parts = lax.axis_size("exp") // FFN_EXPERTS
    capacity = max(4, tok_rows // 64 * 12)
    tokens_in = inputs[0].astype(jnp.float32)
    normed_attn, inverse_attn = rms_forward(tokens_in, attn_gain)
    act_low = normed_attn.astype(jnp.bfloat16)
    projected = jnp.dot(act_low, w_qkv, preferred_element_type=jnp.float32).astype(jnp.bfloat16)
    queries = projected[:, :model_width]
    kv_local = projected[:prompt_local, model_width:]
    own_kv = projected[prompt_local:, model_width:]
    gathered = lax.all_gather(kv_local, "ctx", axis=0, tiled=True)
    row_index = jnp.arange(tok_rows, dtype=jnp.int32)
    query_pos = lax.axis_index("ctx") * prompt_local + row_index
    cont_pos = row_index - prompt_local
    key_index = jnp.arange(prompt_len + CONT_LEN, dtype=jnp.int32)
    in_prompt = key_index[None, :] < prompt_len
    prompt_mask = in_prompt & (key_index[None, :] <= query_pos[:, None])
    cont_mask = in_prompt | (key_index[None, :] - prompt_len <= cont_pos[:, None])
    allowed = jnp.where((row_index < prompt_local)[:, None], prompt_mask, cont_mask)
    all_kv = jnp.concatenate([gathered, own_kv], axis=0)
    heads_out, row_lse = lax.map(
        partial(head_forward, allowed),
        (
            split_heads(queries),
            split_heads(all_kv[:, :model_width]),
            split_heads(all_kv[:, model_width:]),
        ),
    )
    mixed_low = join_heads(heads_out).astype(jnp.bfloat16)
    hidden = tokens_in + jnp.dot(mixed_low, w_out, preferred_element_type=jnp.float32)
    normed_moe, inverse_moe = rms_forward(hidden, moe_gain)
    moe_low = normed_moe.astype(jnp.bfloat16)
    logits = jnp.dot(moe_low, router, preferred_element_type=jnp.float32) + prev_logits[0]
    route_ids = routes[0]
    probs_all = jax.nn.softmax(logits, axis=-1)
    gate_values = jnp.take_along_axis(probs_all, route_ids, axis=-1)
    const_logits = jnp.einsum(
        "td,cda->tca", moe_low, const_gate, preferred_element_type=jnp.float32
    )
    alphas = jax.nn.softmax(const_logits, axis=-1)
    const_out = alphas[..., 0:1] * normed_moe[:, None, :] + alphas[..., 1:2] * const_vec[None]
    slot_index = route_slots(route_ids)
    is_ffn = route_ids < FFN_EXPERTS
    expert_ids = jnp.where(is_ffn, route_ids, FFN_EXPERTS)
    token_ids = jnp.broadcast_to(jnp.arange(tok_rows, dtype=jnp.int32)[:, None], route_ids.shape)
    dispatch = (
        jnp.full((FFN_EXPERTS, capacity), tok_rows, jnp.int32)
        .at[expert_ids, slot_index]
        .set(token_ids, mode="drop")
    )
    padded = jnp.concatenate([moe_low, jnp.zeros((1, model_width), jnp.bfloat16)], axis=0)
    dealt = padded[dispatch]
    received = lax.all_to_all(
        jnp.repeat(dealt, split_parts, axis=0), "exp", split_axis=0, concat_axis=0, tiled=True
    )
    leading = received.shape[:2]
    flat_rows = received.reshape(-1, model_width)
    gate_pre = jnp.dot(flat_rows, w_gate[0], preferred_element_type=jnp.float32)
    up_pre = jnp.dot(flat_rows, w_up[0], preferred_element_type=jnp.float32)
    inner_act = (jax.nn.silu(gate_pre) * up_pre).astype(jnp.bfloat16)
    partial_out = jnp.dot(inner_act, w_down[0], preferred_element_type=jnp.float32).astype(
        jnp.bfloat16
    )
    partial_out, kept_rows, gate_kept, up_kept = (
        partial_out.reshape(leading + (model_width,)),
        received,
        gate_pre.reshape(leading + (-1,)),
        up_pre.reshape(leading + (-1,)),
    )
    returned = lax.all_to_all(partial_out, "exp", split_axis=0, concat_axis=0, tiled=True)
    expert_out = jnp.sum(
        returned.reshape(FFN_EXPERTS, split_parts, capacity, model_width).astype(jnp.float32),
        axis=1,
    )
    position = expert_ids * capacity + slot_index
    picked = jnp.where(
        is_ffn[..., None], expert_out.reshape(-1, model_width)[jnp.where(is_ffn, position, 0)], 0.0
    )
    selected = picked + jnp.where(
        (route_ids == FFN_EXPERTS + 1)[..., None], normed_moe[:, None, :], 0.0
    )
    selected = selected + jnp.where(
        (route_ids == FFN_EXPERTS + 2)[..., None], const_out[:, 0:1], 0.0
    )
    selected = selected + jnp.where(
        (route_ids == FFN_EXPERTS + 3)[..., None], const_out[:, 1:2], 0.0
    )
    mixed_out = (hidden + jnp.sum(gate_values[..., None] * selected, axis=1)).astype(jnp.bfloat16)[
        None
    ]
    upstream = out_grad[0].astype(jnp.float32)
    d_gate_values = jnp.sum(upstream[:, None, :] * selected, axis=-1)
    weighted = gate_values[..., None] * upstream[:, None, :]
    flat_position = jnp.where(is_ffn, position, FFN_EXPERTS * capacity)
    d_expert = (
        jnp.zeros((FFN_EXPERTS * capacity, model_width), jnp.float32)
        .at[flat_position]
        .set(weighted, mode="drop")
    )
    d_expert_low = d_expert.astype(jnp.bfloat16).reshape(FFN_EXPERTS, capacity, model_width)
    incoming_grad = lax.all_to_all(
        jnp.repeat(d_expert_low, split_parts, axis=0),
        "exp",
        split_axis=0,
        concat_axis=0,
        tiled=True,
    )
    flat_rows = kept_rows.reshape(-1, model_width)
    flat_grad = incoming_grad.reshape(-1, model_width)
    gate_flat = gate_kept.reshape(flat_rows.shape[0], -1)
    up_flat = up_kept.reshape(flat_rows.shape[0], -1)
    sigmoid_gate = jax.nn.sigmoid(gate_flat)
    silu_gate = gate_flat * sigmoid_gate
    inner_act = (silu_gate * up_flat).astype(jnp.bfloat16)
    d_inner = jnp.dot(flat_grad, w_down[0].T, preferred_element_type=jnp.float32)
    d_w_down_local = jnp.dot(inner_act.T, flat_grad, preferred_element_type=jnp.float32)
    d_gate_pre = (
        d_inner * up_flat * sigmoid_gate * (1.0 + gate_flat * (1.0 - sigmoid_gate))
    ).astype(jnp.bfloat16)
    d_up_pre = (d_inner * silu_gate).astype(jnp.bfloat16)
    d_w_gate_local = jnp.dot(flat_rows.T, d_gate_pre, preferred_element_type=jnp.float32)
    d_w_up_local = jnp.dot(flat_rows.T, d_up_pre, preferred_element_type=jnp.float32)
    gate_up_local = jnp.stack([d_w_gate_local, d_w_up_local])[None]
    down_local = d_w_down_local[None]
    d_rows = jnp.dot(d_gate_pre, w_gate[0].T, preferred_element_type=jnp.float32) + jnp.dot(
        d_up_pre, w_up[0].T, preferred_element_type=jnp.float32
    )
    row_grads = lax.all_to_all(
        d_rows.reshape(kept_rows.shape).astype(jnp.bfloat16),
        "exp",
        split_axis=0,
        concat_axis=0,
        tiled=True,
    ).astype(jnp.float32)
    d_dispatch = jnp.sum(row_grads.reshape(FFN_EXPERTS, split_parts, capacity, model_width), axis=1)
    expert_sums = (
        lax.psum_scatter(
            gate_up_local.astype(jnp.bfloat16), "ctx", scatter_dimension=2, tiled=True
        ).astype(jnp.float32),
        lax.psum_scatter(
            down_local.astype(jnp.bfloat16), "ctx", scatter_dimension=1, tiled=True
        ).astype(jnp.float32),
    )
    total_gate_up = expert_sums[0][0]
    total_down = expert_sums[1][0]
    d_moe_low = (
        jnp.zeros((tok_rows + 1, model_width), jnp.float32).at[dispatch].add(d_dispatch)[:tok_rows]
    )
    onehot_routes = (route_ids[..., None] == jnp.arange(ALL_EXPERTS, dtype=jnp.int32)).astype(
        jnp.float32
    )
    d_probs = jnp.sum(onehot_routes * d_gate_values[..., None], axis=1)
    d_logits = probs_all * (d_probs - jnp.sum(probs_all * d_probs, axis=-1, keepdims=True))
    moe_wide = moe_low.astype(jnp.float32)
    d_router = jnp.dot(moe_wide.T, d_logits, precision=highest)
    d_moe_low = d_moe_low + jnp.dot(d_logits, router.astype(jnp.float32).T, precision=highest)
    const_weight = jnp.stack(
        [
            jnp.sum(jnp.where(route_ids == FFN_EXPERTS + 2 + offset, gate_values, 0.0), axis=1)
            for offset in range(2)
        ],
        axis=1,
    )
    d_const_out = const_weight[..., None] * upstream[:, None, :]
    d_alpha = jnp.stack(
        [
            jnp.sum(d_const_out * normed_moe[:, None, :], axis=-1),
            jnp.sum(d_const_out * const_vec[None], axis=-1),
        ],
        axis=-1,
    )
    d_const_logits = alphas * (d_alpha - jnp.sum(alphas * d_alpha, axis=-1, keepdims=True))
    d_const_gate = jnp.einsum("td,tca->cda", moe_wide, d_const_logits, precision=highest)
    d_moe_low = d_moe_low + jnp.einsum(
        "tca,cda->td", d_const_logits, const_gate.astype(jnp.float32), precision=highest
    )
    d_const_vec = jnp.sum(d_const_out * alphas[..., 1:2], axis=0)
    copy_weight = jnp.sum(jnp.where(route_ids == FFN_EXPERTS + 1, gate_values, 0.0), axis=1)
    d_normed = (
        d_moe_low
        + copy_weight[:, None] * upstream
        + jnp.sum(d_const_out * alphas[..., 0:1], axis=1)
    )
    d_hidden_norm, d_moe_gain = rms_backward(hidden, inverse_moe, moe_gain, d_normed)
    d_hidden = upstream + d_hidden_norm
    d_attn_low = d_hidden.astype(jnp.bfloat16)
    d_w_out = jnp.dot(mixed_low.T, d_attn_low, preferred_element_type=jnp.float32)
    d_mixed = jnp.dot(d_attn_low, w_out.T, preferred_element_type=jnp.float32).astype(jnp.bfloat16)
    kv_back = lax.all_gather(kv_local, "ctx", axis=0, tiled=True)
    all_back = jnp.concatenate([kv_back, own_kv], axis=0)
    d_heads = lax.map(
        partial(head_backward, allowed),
        (
            split_heads(queries),
            split_heads(all_back[:, :model_width]),
            split_heads(all_back[:, model_width:]),
            split_heads(d_mixed),
            row_lse,
        ),
    )
    d_queries = join_heads(d_heads[0])
    kv_grad = jnp.concatenate([join_heads(d_heads[1]), join_heads(d_heads[2])], axis=-1)
    own_prompt_grad = lax.psum_scatter(
        kv_grad[:prompt_len].astype(jnp.bfloat16), "ctx", scatter_dimension=0, tiled=True
    ).astype(jnp.float32)
    kv_rows = jnp.concatenate([own_prompt_grad, kv_grad[prompt_len:]], axis=0)
    d_projected = jnp.concatenate([d_queries, kv_rows], axis=-1).astype(jnp.bfloat16)
    d_w_qkv = jnp.dot(act_low.T, d_projected, preferred_element_type=jnp.float32)
    d_act = jnp.dot(d_projected, w_qkv.T, preferred_element_type=jnp.float32)
    d_tokens_norm, d_attn_gain = rms_backward(tokens_in, inverse_attn, attn_gain, d_act)
    d_inputs = (d_hidden + d_tokens_norm)[None]
    dense_sums = lax.psum(
        (d_attn_gain, d_w_qkv, d_w_out, d_moe_gain, d_router, d_const_gate, d_const_vec),
        ("ctx", "exp"),
    )
    return (
        mixed_out,
        d_inputs,
        d_logits[None],
        dense_sums[0],
        dense_sums[1],
        dense_sums[2],
        dense_sums[3],
        dense_sums[4],
        dense_sums[5],
        dense_sums[6],
        total_gate_up[0][None],
        total_gate_up[1][None],
        total_down[None],
    )


def solution(mesh):
    return jax.shard_map(
        body,
        mesh=mesh,
        in_specs=(
            P("ctx", "exp", None),
            P("ctx", "exp", None),
            P("ctx", "exp", None),
            P(),
            P(),
            P(),
            P(),
            P(),
            P(),
            P(),
            P("exp", None, None),
            P("exp", None, None),
            P("exp", None, None),
            P("ctx", "exp", None),
        ),
        out_specs=(
            P("ctx", "exp", None),
            P("ctx", "exp", None),
            P("ctx", "exp", None),
            P(),
            P(),
            P(),
            P(),
            P(),
            P(),
            P(),
            P("exp", "ctx", None),
            P("exp", "ctx", None),
            P("exp", "ctx", None),
        ),
        check_vma=False,
    )
```

profile of v0, /device:TPU:0, one launch (start us, length us, event | category | flops | bytes accessed | tf_op | source)
XLA Modules:
  0.0 1069.1 jit_solution(18259728918760266135)
XLA Ops:
  26.2 7.3 reduce-window.6
  91.6 130.8 %while.28 = (s32[]{:T(128)}, bf16[12,768,64]{1,2,0:T(8,128)(2,1)}, f32[12,768]{1,0:T(8,128)}, bf16[12,768,64]{2,1,0:T(8,128)(2,1)}, bf16[12,1536,64]{2,1,0:T(8,1...) while((s32[]{:T(128)}, bf16[12,768,64]{1,2,0:T(8,128)(2,1)}, ...), condition=%wide.region_4.5_spmd.clone, body=%wide.region_1.4_spmd.clone.sunk | while | flops 317324544 | bytes 34315476 | solution.py:125
  230.3 7.2 gather_fusion
  237.4 6.6 all-to-all-start
  252.5 11.5 %gather_fusion.2 = f32[1536]{0:T(1024)S(1)} fusion(f32[768,12]{0,1:T(8,128)} %fusion.115, s32[1536]{0:T(1024)S(1)} %reshape.454), kind=kCustom, calls=%fused_computation.2 | custom fusion | bytes 24576 | tf_op jit(solution)/shard_map/jit(take_along_axis)/gather | solution.py:140
  268.5 7.0 broadcast_multiply_fusion
  275.5 6.9 reshape.464
  282.4 9.7 scatter_custom_fusion
  313.2 10.1 fusion.65
  323.3 7.7 fusion.69
  331.0 12.1 %all-to-all-done.2 = bf16[8,144,768]{2,1,0:T(8,128)(2,1)} async-done(((bf16[8,144,768]{2,1,0:T(8,128)(2,1)}), bf16[8,144,768]{2,1,0:T(8,128)(2,1)}, u32[]{:S(2)}, u32[]{:S(2)}) %all-to-all-start.2) | async-done | bytes 1769504 | tf_op jit(solution)/shard_map/all_to_all | solution.py:205
  343.1 16.6 %multiply_convert_fusion.1 = (bf16[1152,2048]{1,0:T(8,128)(2,1)}, bf16[1152,2048]{1,0:T(8,128)(2,1)}, bf16[1152,2048]{1,0:T(8,128)(2,1)}) fusion(f32[1152,2048]{1,0:T(8,128)} %fusion.69, f32[1152,2048]{1,0:T(8,128)} %fusion.65, bf16[1152,768]{1,0:T(8,128)(2,1)} %bitcast.27, bf16[1,2048,768]{2,1,0:T(8,128)(2,1)} %param.30), kind=kOutput, calls=%fused_computation.66 | convolution fusion | flops 3659268096 | bytes 37945344 | tf_op jit(solution)/shard_map/dot_general | solution.py:219
  359.7 7.4 convolution_convert_fusion.4
  388.9 6.8 fusion.67
  395.8 7.5 fusion.60
  403.3 10.5 all-to-all-done.1
  421.9 8.9 gather_fusion.1
  430.7 6.7 reshape.447
  437.4 38.7 %fusion.57 = (f32[2,768]{1,0:T(2,128)}, f32[768,768]{1,0:T(8,128)}, f32[768,2]{1,0:T(8,128)}, f32[768,2]{1,0:T(8,128)}, f32[768,768]{1,0:T(8,128)}, /*index=5*/f32[768,2]{1,0:T(8,128)}) fusion(f32[768,2]{1,0:T(8,128)} %copy.148, f32[768,768]{1,0:T(8,128)} %bitcast_convert_fusion.1, f32[768,2]{1,0:T(8,128)} %bitcast.275, f32[768,2]{1,0:T(8,128)} %bitcast.273, ...), kind=kLoop, calls=%fused_computation.86 | loop fusion | flops 22407168 | bytes 18935808 | tf_op jit(solution)/shard_map/reduce_sum | solution.py:281
  488.5 13.2 %scatter_custom_fusion.1 = f32[769,768]{1,0:T(8,128)} fusion(s32[1152]{0:T(1024)} %copy-done.33, bf16[1152,768]{1,0:T(8,128)(2,1)} %bitcast.65, f32[]{:T(128)} %constant.56.clone.1), kind=kCustom, calls=%fused_computation.95 | custom fusion | flops 1769472 | bytes 4132352 | tf_op jit(solution)/shard_map/scatter-add | solution.py:251
  501.8 7.0 multiply_reduce_fusion.3
  517.6 168.1 %while.29 = (s32[]{:T(128)}, bf16[12,768,64]{1,2,0:T(8,128)(2,1)}, bf16[12,1536,64]{1,2,0:T(8,128)(2,1)}, bf16[12,1536,64]{1,2,0:T(8,128)(2,1)}, bf16[12,768,64]...) while((s32[]{:T(128)}, bf16[12,768,64]{1,2,0:T(8,128)(2,1)}, ...), condition=%wide.region_30.31_spmd.clone, body=%wide.region_28.30_spmd.clone.sunk | while | flops 772816128 | bytes 38401196 | solution.py:295
  690.7 8.9 fusion.73
  699.6 7.2 fusion.71
  706.8 7.4 fusion.72
  723.0 12.9 %reduce-scatter.4.cloned.1.call-done = bf16[256,1536]{0,1:T(8,128)(2,1)} async-done(((bf16[1024,1536]{0,1:T(8,128)(2,1)}), bf16[256,1536]{0,1:T(8,128)(2,1)}) %reduce-scatter.4.cloned.1.call-update) | async-done | bytes 786448 | tf_op jit(solution)/shard_map/reduce_scatter | solution.py:307
  735.9 8.5 fusion.90
  750.9 31.9 %reduce-scatter.8.cloned.1.call-done = bf16[1,512,768]{2,1,0:T(8,128)(2,1)} async-done(((bf16[1,2048,768]{2,1,0:T(8,128)(2,1)}), bf16[1,512,768]{2,1,0:T(8,128)(2,1)}) %reduce-scatter.8.cloned.1.call-update) | async-done | bytes 786448 | tf_op jit(solution)/shard_map/reduce_scatter | solution.py:244
  785.4 6.9 fusion.84
  792.3 41.7 %all-reduce.1 = (f32[768]{0:T(1024)}, f32[768]{0:T(1024)}, f32[768,12]{0,1:T(8,128)}, f32[2,768,2]{1,2,0:T(2,128)}, f32[2,768]{1,0:T(2,128)}) all-reduce(f32[768]{0:T(1024)} %get-tuple-element.381, f32[768]{0:T(1024)} %get-tuple-element.377, f32[768,12]{0,1:T(8,128)} %fusion.130, ...), channel_id=1, replica_groups=mesh['ctx'=4,'exp'=8] {'ctx','exp'}, use_global_device_ids=true, to_apply=%region_34.35 | all-reduce | flops 15360 | bytes 122880 | tf_op jit(solution)/shard_map/psum | solution.py:316
  840.5 16.3 %reduce-scatter.6.cloned.1.call-done = bf16[1,2,192,2048]{3,2,1,0:T(8,128)(2,1)} async-done(((bf16[1,2,768,2048]{3,2,1,0:T(8,128)(2,1)}), bf16[1,2,192,2048]{3,2,1,0:T(8,128)(2,1)}) %reduce-scatter.6.cloned.1.call-update) | async-done | bytes 1572880 | tf_op jit(solution)/shard_map/reduce_scatter | solution.py:241
  860.4 194.0 %all-reduce.5.cloned.1.call-done = (f32[768,2304]{1,0:T(8,128)}, f32[768,768]{1,0:T(8,128)}) async-done(((f32[768,2304]{1,0:T(8,128)}, f32[768,768]{1,0:T(8,128)}), (f32[768,2304]{1,0:T(8,128)}, f32[768,768]{1,0:T(8,128)})) %all-reduce.5.cloned.1.call-update) | async-done | bytes 9437200 | tf_op jit(solution)/shard_map/psum | solution.py:316
  (466 shorter events, 509.1 us)
Async XLA Ops:
  7.2 58.8 %all-gather.2.cloned.1.call-start = ((), (), s32[]{:S(2)}) async-start(), calls=%async_computation.7 | async-start | bytes 3932160 | tf_op jit(solution)/shard_map/all_gather | solution.py:115
  9.6 4.9 copy-start.36
  57.5 7.3 copy-start.33
  131.0 4.2 copy-start.42
  152.8 4.2 copy-start.42
  174.6 4.2 copy-start.42
  196.4 4.2 copy-start.42
  237.4 58.0 %all-to-all-start = ((bf16[8,144,768]{2,1,0:T(8,128)(2,1)}), bf16[8,144,768]{2,1,0:T(8,128)(2,1)}, u32[]{:S(2)}, u32[]{:S(2)}) async-start(bf16[8,144,768]{2,1,0:T(8,128)(2,1)} %bitcast.269), calls=%async_computation | async-start | bytes 3538944 | tf_op jit(solution)/shard_map/all_to_all | solution.py:157
  295.4 47.7 %all-to-all-start.2 = ((bf16[8,144,768]{2,1,0:T(8,128)(2,1)}), bf16[8,144,768]{2,1,0:T(8,128)(2,1)}, u32[]{:S(2)}, u32[]{:S(2)}) async-start(bf16[8,144,768]{2,1,0:T(8,128)(2,1)} %bitcast.270), calls=%async_computation.2 | async-start | bytes 3538944 | tf_op jit(solution)/shard_map/all_to_all | solution.py:205
  308.0 15.3 %copy-start.28 = (f32[768,2]{0,1:T(2,128)}, f32[768,2]{0,1:T(2,128)S(1)}, u32[]{:S(2)}) copy-start(f32[768,2]{0,1:T(2,128)S(1)} %get-tuple-element.485) | copy-start | bytes 18436
  313.2 10.1 copy-start.47
  343.1 16.6 %copy-start.46 = (bf16[1,2048,768]{2,1,0:T(8,128)(2,1)S(1)}, bf16[1,2048,768]{2,1,0:T(8,128)(2,1)}, u32[]{:S(2)}) copy-start(bf16[1,2048,768]{2,1,0:T(8,128)(2,1)} %param.30) | copy-start | bytes 9437188
  367.1 4.6 copy-start.34
  367.1 46.7 %all-to-all-start.1 = ((bf16[8,144,768]{2,1,0:T(8,128)(2,1)}), bf16[8,144,768]{2,1,0:T(8,128)(2,1)}, u32[]{:S(2)}, u32[]{:S(2)}) async-start(bf16[8,144,768]{2,1,0:T(8,128)(2,1)} %bitcast.277), calls=%async_computation.1 | async-start | bytes 3538944 | tf_op jit(solution)/shard_map/all_to_all | solution.py:174
  388.9 6.9 copy-start.48
  413.8 74.7 %all-to-all-start.3 = ((bf16[8,144,768]{2,1,0:T(8,128)(2,1)}), bf16[8,144,768]{2,1,0:T(8,128)(2,1)}, u32[]{:S(2)}, u32[]{:S(2)}) async-start(bf16[8,144,768]{2,1,0:T(8,128)(2,1)} %bitcast.276), calls=%async_computation.3 | async-start | bytes 3538944 | tf_op jit(solution)/shard_map/all_to_all | solution.py:232
  418.1 317.8 %reduce-scatter.4.cloned.1.call-start = ((), (), s32[]{:S(2)}) async-start(), calls=%async_computation.8 | async-start | bytes 3932160 | tf_op jit(solution)/shard_map/reduce_scatter | solution.py:307
  437.4 45.5 %copy-start.21 = (f32[768]{0:T(1024)S(1)}, f32[768]{0:T(1024)}, u32[]{:S(2)}) copy-start(f32[768]{0:T(1024)} %copy-done.20) | copy-start | bytes 9220
  437.4 47.8 %copy-start.19 = (f32[768,2,2]{0,2,1:T(2,128)S(1)}, f32[768,2,2]{0,2,1:T(2,128)}, u32[]{:S(2)}) copy-start(f32[768,2,2]{0,2,1:T(2,128)} %copy-done.18) | copy-start | bytes 36868
  488.5 13.2 %copy-start.26 = (f32[768]{0:T(1024)S(1)}, f32[768]{0:T(1024)}, u32[]{:S(2)}) copy-start(f32[768]{0:T(1024)} %copy-done.25) | copy-start | bytes 9220
  501.7 7.1 copy-start.5
  501.8 7.1 copy-start.6
  501.8 7.0 copy-start.10
  501.8 7.0 copy-start.31
  501.8 7.0 copy-start.38
  690.4 92.4 %reduce-scatter.8.cloned.1.call-start = ((), (), s32[]{:S(2)}) async-start(), calls=%async_computation.10 | async-start | bytes 3932160 | tf_op jit(solution)/shard_map/reduce_scatter | solution.py:244
  699.6 157.2 %reduce-scatter.6.cloned.1.call-start = ((), (), s32[]{:S(2)}) async-start(), calls=%async_computation.9 | async-start | bytes 7864320 | tf_op jit(solution)/shard_map/reduce_scatter | solution.py:241
  717.4 337.0 %all-reduce.5.cloned.1.call-start = ((), (), s32[]{:S(2)}) async-start(), calls=%async_computation.11 | async-start | bytes 18874368 | tf_op jit(solution)/shard_map/psum | solution.py:316
  720.5 15.4 %copy-start.37 = (f32[768]{0:T(1024)S(1)}, f32[768]{0:T(1024)}, u32[]{:S(2)}) copy-start(f32[768]{0:T(1024)} %copy-done.36) | copy-start | bytes 9220
  785.4 6.9 copy-start.29
  785.4 49.4 %copy-start.35 = (f32[768]{0:T(1024)S(1)}, f32[768]{0:T(1024)}, u32[]{:S(2)}) copy-start(f32[768]{0:T(1024)} %get-tuple-element.477) | copy-start | bytes 9220
  1054.4 6.6 copy-start.14
  (71 other events, 185.8 us)
Sparse Core Ops, SparseCore 0:
  17.3 46.6 all-gather.1
  690.6 45.2 reduce-scatter.3
  738.9 43.9 reduce-scatter.7
  785.7 71.0 reduce-scatter.5
  863.2 191.2 all-reduce.4
where the time goes:
time: 1080 us; the launch traced here: 1070 us
  matrix products  367 us (34%)
  waiting for transfers between devices  278 us (26%)
  local copies, waits for them, and re-layouts  200 us (19%)
  other arithmetic  146 us (14%)
  blocking collectives  41.7 us (4%)
  starting transfers between devices  21.9 us (2%)
  between operations  14.5 us (1%)
    psum x1, waiting for transfers between devices, body(): lax.psum((d_attn_gain, d_w_qkv, d_w_out, d_moe_gain, d_router, d_const_ga...  194 us
    dot_general x12, matrix products, head_forward(): jnp.einsum('qk,kd->qd', weights_soft, value_rows, preferred_element_type=...  50.2 us
    dot_general x12, matrix products, head_backward(): jnp.einsum('qd,kd->qk', queries, key_rows, preferred_element_type=jnp.flo...  48.2 us
    unnamed x106, local copies, waits for them, and re-layouts  45.2 us
    psum x1, blocking collectives, body(): lax.psum((d_attn_gain, d_w_qkv, d_w_out, d_moe_gain, d_router, d_const_ga...  41.7 us
    reduce_sum x1, other arithmetic, body(): d_const_vec = jnp.sum(d_const_out * alphas[..., 1:2], axis=0)  38.7 us
    dot_general x12, matrix products, head_forward(): jnp.einsum('qd,kd->qk', queries, key_rows, preferred_element_type=jnp.flo...  38.3 us
    reduce_scatter x1, waiting for transfers between devices, body(): lax.psum_scatter(down_local.astype(jnp.bfloat16), 'ctx', scatter_dimensio...  31.9 us
  transfers between devices with their start and end apart: 9, of which 6 were waited for; matrix products, arithmetic and copies ran while one was open for 28% of the time, Pallas kernels for 0%

commit v1 on v0

--- a/solution.py
+++ b/solution.py
@@ -314,8 +314,10 @@
     d_tokens_norm, d_attn_gain = rms_backward(tokens_in, inverse_attn, attn_gain, d_act)
     d_inputs = (d_hidden + d_tokens_norm)[None]
     dense_sums = lax.psum(
-        (d_attn_gain, d_w_qkv, d_w_out, d_moe_gain, d_router, d_const_gate, d_const_vec),
-        ("ctx", "exp"),
+        lax.psum(
+            (d_attn_gain, d_w_qkv, d_w_out, d_moe_gain, d_router, d_const_gate, d_const_vec), "exp"
+        ),
+        "ctx",
     )
     return (
         mixed_out,

time: 1080 us -> 1280 us (1.19)
  waiting for transfers between devices: 278 us -> 471 us
    psum x0 -> x1, waiting for transfers between devices: none -> 189 us  [body(): lax.psum(lax.psum((d_attn_gain, d_w_qkv, d_w_out, d_moe_gain, d_router, d...]
    reduce_scatter x1, waiting for transfers between devices: 12.9 us -> 39.9 us  [body(): lax.psum_scatter(kv_grad[:prompt_len].astype(jnp.bfloat16), 'ctx', scatte...]
    psum x1, waiting for transfers between devices: 194 us -> 169 us  [body(): lax.psum((d_attn_gain, d_w_qkv, d_w_out, d_moe_gain, d_router, d_const_ga...]
    psum x0 -> x1, blocking collectives: none -> 17.7 us  [body(): lax.psum(lax.psum((d_attn_gain, d_w_qkv, d_w_out, d_moe_gain, d_router, d...]
  transfers between devices with their start and end apart: 9 -> 10, of which waited for: 6 -> 7; matrix products, arithmetic and copies ran while one was open for 28% -> 23% of each run, Pallas kernels for 0% -> 0%
where the time goes in v1:
time: 1280 us; the launch traced here: 1270 us
  waiting for transfers between devices  471 us (37%)
  matrix products  367 us (29%)
  local copies, waits for them, and re-layouts  200 us (16%)
  other arithmetic  145 us (11%)
  blocking collectives  48.5 us (4%)
  starting transfers between devices  22.2 us (2%)
  between operations  14.9 us (1%)
    psum x1, waiting for transfers between devices, body(): lax.psum(lax.psum((d_attn_gain, d_w_qkv, d_w_out, d_moe_gain, d_router, d...  189 us
    psum x1, waiting for transfers between devices, body(): lax.psum((d_attn_gain, d_w_qkv, d_w_out, d_moe_gain, d_router, d_const_ga...  169 us
    dot_general x12, matrix products, head_forward(): jnp.einsum('qk,kd->qd', weights_soft, value_rows, preferred_element_type=...  50.2 us
    dot_general x12, matrix products, head_backward(): jnp.einsum('qd,kd->qk', queries, key_rows, preferred_element_type=jnp.flo...  48.2 us
    unnamed x106, local copies, waits for them, and re-layouts  45.2 us
    reduce_scatter x1, waiting for transfers between devices, body(): lax.psum_scatter(down_local.astype(jnp.bfloat16), 'ctx', scatter_dimensio...  40.5 us
    reduce_scatter x1, waiting for transfers between devices, body(): lax.psum_scatter(kv_grad[:prompt_len].astype(jnp.bfloat16), 'ctx', scatte...  39.9 us
    reduce_sum x1, other arithmetic, body(): d_const_vec = jnp.sum(d_const_out * alphas[..., 1:2], axis=0)  38.7 us
  transfers between devices with their start and end apart: 10, of which 7 were waited for; matrix products, arithmetic and copies ran while one was open for 23% of the time, Pallas kernels for 0%

profile of v1, /device:TPU:0, one launch (start us, length us, event | category | flops | bytes accessed | tf_op | source)
XLA Modules:
  0.0 1268.9 jit_solution(6101374258671898628)
XLA Ops:
  26.2 7.3 reduce-window.6
  91.6 130.8 %while.28 = (s32[]{:T(128)}, bf16[12,768,64]{1,2,0:T(8,128)(2,1)}, f32[12,768]{1,0:T(8,128)}, bf16[12,768,64]{2,1,0:T(8,128)(2,1)}, bf16[12,1536,64]{2,1,0:T(8,1...) while((s32[]{:T(128)}, bf16[12,768,64]{1,2,0:T(8,128)(2,1)}, ...), condition=%wide.region_4.5_spmd.clone, body=%wide.region_1.4_spmd.clone.sunk | while | flops 317324544 | bytes 34315476 | solution.py:125
  230.3 7.2 gather_fusion
  252.5 11.5 gather_fusion.2
  268.5 7.0 broadcast_multiply_fusion
  275.5 6.9 reshape.464
  282.4 9.7 scatter_custom_fusion
  313.2 10.1 fusion.65
  323.3 7.7 fusion.69
  331.0 12.1 all-to-all-done.2
  343.1 16.6 %multiply_convert_fusion.1 = (bf16[1152,2048]{1,0:T(8,128)(2,1)}, bf16[1152,2048]{1,0:T(8,128)(2,1)}, bf16[1152,2048]{1,0:T(8,128)(2,1)}) fusion(f32[1152,2048]{1,0:T(8,128)} %fusion.69, f32[1152,2048]{1,0:T(8,128)} %fusion.65, bf16[1152,768]{1,0:T(8,128)(2,1)} %bitcast.27, bf16[1,2048,768]{2,1,0:T(8,128)(2,1)} %param.30), kind=kOutput, calls=%fused_computation.66 | convolution fusion | flops 3659268096 | bytes 37945344 | tf_op jit(solution)/shard_map/dot_general | solution.py:219
  359.7 7.4 convolution_convert_fusion.4
  388.9 6.8 fusion.67
  395.8 7.5 fusion.60
  403.3 10.5 all-to-all-done.1
  421.9 8.9 gather_fusion.1
  437.4 38.7 %fusion.57 = (f32[2,768]{1,0:T(2,128)}, f32[768,768]{1,0:T(8,128)}, f32[768,2]{1,0:T(8,128)}, f32[768,2]{1,0:T(8,128)}, f32[768,768]{1,0:T(8,128)}, /*index=5*/f32[768,2]{1,0:T(8,128)}) fusion(f32[768,2]{1,0:T(8,128)} %copy.148, f32[768,768]{1,0:T(8,128)} %bitcast_convert_fusion.1, f32[768,2]{1,0:T(8,128)} %bitcast.275, f32[768,2]{1,0:T(8,128)} %bitcast.273, ...), kind=kLoop, calls=%fused_computation.86 | loop fusion | flops 22407168 | bytes 18935808 | tf_op jit(solution)/shard_map/reduce_sum | solution.py:281
  488.5 13.2 %scatter_custom_fusion.1 = f32[769,768]{1,0:T(8,128)} fusion(s32[1152]{0:T(1024)} %copy-done.33, bf16[1152,768]{1,0:T(8,128)(2,1)} %bitcast.65, f32[]{:T(128)} %constant.56.clone.1), kind=kCustom, calls=%fused_computation.95 | custom fusion | flops 1769472 | bytes 4132352 | tf_op jit(solution)/shard_map/scatter-add | solution.py:251
  501.8 7.0 multiply_reduce_fusion.3
  517.6 168.1 %while.29 = (s32[]{:T(128)}, bf16[12,768,64]{1,2,0:T(8,128)(2,1)}, bf16[12,1536,64]{1,2,0:T(8,128)(2,1)}, bf16[12,1536,64]{1,2,0:T(8,128)(2,1)}, bf16[12,768,64]...) while((s32[]{:T(128)}, bf16[12,768,64]{1,2,0:T(8,128)(2,1)}, ...), condition=%wide.region_30.31_spmd.clone, body=%wide.region_28.30_spmd.clone.sunk | while | flops 772816128 | bytes 38401196 | solution.py:295
  696.0 39.9 %reduce-scatter.4.cloned.1.call-done = bf16[256,1536]{0,1:T(8,128)(2,1)} async-done(((bf16[1024,1536]{0,1:T(8,128)(2,1)}), bf16[256,1536]{0,1:T(8,128)(2,1)}) %reduce-scatter.4.cloned.1.call-update) | async-done | bytes 786448 | tf_op jit(solution)/shard_map/reduce_scatter | solution.py:307
  735.9 8.5 fusion.90
  744.5 8.9 fusion.73
  753.7 7.2 fusion.71
  760.9 7.2 fusion.72
  771.6 168.7 %all-reduce.8.cloned.1.call-done = (f32[768,2304]{1,0:T(8,128)}, f32[768,768]{1,0:T(8,128)}) async-done(((f32[768,2304]{1,0:T(8,128)}, f32[768,768]{1,0:T(8,128)}), (f32[768,2304]{1,0:T(8,128)}, f32[768,768]{1,0:T(8,128)})) %all-reduce.8.cloned.1.call-update) | async-done | bytes 9437200 | tf_op jit(solution)/shard_map/psum | solution.py:317
  946.8 40.5 %reduce-scatter.8.cloned.1.call-done = bf16[1,512,768]{2,1,0:T(8,128)(2,1)} async-done(((bf16[1,2048,768]{2,1,0:T(8,128)(2,1)}), bf16[1,512,768]{2,1,0:T(8,128)(2,1)}) %reduce-scatter.8.cloned.1.call-update) | async-done | bytes 786448 | tf_op jit(solution)/shard_map/reduce_scatter | solution.py:244
  989.8 6.9 fusion.84
  996.7 30.8 %all-reduce.1 = (f32[768]{0:T(1024)}, f32[768]{0:T(1024)}, f32[768,12]{0,1:T(8,128)}, f32[2,768,2]{1,2,0:T(2,128)}, f32[2,768]{1,0:T(2,128)}) all-reduce(f32[768]{0:T(1024)} %get-tuple-element.381, f32[768]{0:T(1024)} %get-tuple-element.377, f32[768,12]{0,1:T(8,128)} %fusion.130, ...), channel_id=1, replica_groups=mesh['ctx'=4,'exp'=8] {'exp'}, use_global_device_ids=true, to_apply=%region_34.35 | all-reduce | flops 15360 | bytes 122880 | tf_op jit(solution)/shard_map/psum | solution.py:317
  1027.5 17.7 %all-reduce.3 = (f32[768]{0:T(1024)}, f32[768]{0:T(1024)}, f32[768,12]{0,1:T(8,128)}, f32[2,768,2]{1,2,0:T(2,128)}, f32[2,768]{1,0:T(2,128)}) all-reduce(f32[768]{0:T(1024)} %get-tuple-element.442, f32[768]{0:T(1024)} %get-tuple-element.443, f32[768,12]{0,1:T(8,128)} %get-tuple-element.444, ...), channel_id=1, replica_groups=mesh['ctx'=4,'exp'=8] {'ctx'}, use_global_device_ids=true, to_apply=%region_35.36 | all-reduce | flops 15360 | bytes 122880 | tf_op jit(solution)/shard_map/psum | solution.py:316
  1050.6 10.5 reduce-scatter.6.cloned.1.call-done
  1064.8 189.0 %all-reduce.10.cloned.1.call-done = (f32[768,2304]{1,0:T(8,128)}, f32[768,768]{1,0:T(8,128)}) async-done(((f32[768,2304]{1,0:T(8,128)}, f32[768,768]{1,0:T(8,128)}), (f32[768,2304]{1,0:T(8,128)}, f32[768,768]{1,0:T(8,128)})) %all-reduce.10.cloned.1.call-update) | async-done | bytes 9437200 | tf_op jit(solution)/shard_map/psum | solution.py:316
  (470 shorter events, 521.5 us)
Async XLA Ops:
  7.2 58.8 %all-gather.2.cloned.1.call-start = ((), (), s32[]{:S(2)}) async-start(), calls=%async_computation.7 | async-start | bytes 3932160 | tf_op jit(solution)/shard_map/all_gather | solution.py:115
  9.6 4.9 copy-start.36
  57.5 7.3 copy-start.33
  141.9 4.2 copy-start.42
  163.7 4.2 copy-start.42
  207.3 4.2 copy-start.42
  237.5 58.0 %all-to-all-start = ((bf16[8,144,768]{2,1,0:T(8,128)(2,1)}), bf16[8,144,768]{2,1,0:T(8,128)(2,1)}, u32[]{:S(2)}, u32[]{:S(2)}) async-start(bf16[8,144,768]{2,1,0:T(8,128)(2,1)} %bitcast.269), calls=%async_computation | async-start | bytes 3538944 | tf_op jit(solution)/shard_map/all_to_all | solution.py:157
  295.4 47.7 %all-to-all-start.2 = ((bf16[8,144,768]{2,1,0:T(8,128)(2,1)}), bf16[8,144,768]{2,1,0:T(8,128)(2,1)}, u32[]{:S(2)}, u32[]{:S(2)}) async-start(bf16[8,144,768]{2,1,0:T(8,128)(2,1)} %bitcast.270), calls=%async_computation.2 | async-start | bytes 3538944 | tf_op jit(solution)/shard_map/all_to_all | solution.py:205
  308.0 15.3 %copy-start.28 = (f32[768,2]{0,1:T(2,128)}, f32[768,2]{0,1:T(2,128)S(1)}, u32[]{:S(2)}) copy-start(f32[768,2]{0,1:T(2,128)S(1)} %get-tuple-element.492) | copy-start | bytes 18436
  313.2 10.1 copy-start.47
  343.1 16.6 %copy-start.46 = (bf16[1,2048,768]{2,1,0:T(8,128)(2,1)S(1)}, bf16[1,2048,768]{2,1,0:T(8,128)(2,1)}, u32[]{:S(2)}) copy-start(bf16[1,2048,768]{2,1,0:T(8,128)(2,1)} %param.30) | copy-start | bytes 9437188
  367.1 4.6 copy-start.34
  367.1 46.7 %all-to-all-start.1 = ((bf16[8,144,768]{2,1,0:T(8,128)(2,1)}), bf16[8,144,768]{2,1,0:T(8,128)(2,1)}, u32[]{:S(2)}, u32[]{:S(2)}) async-start(bf16[8,144,768]{2,1,0:T(8,128)(2,1)} %bitcast.277), calls=%async_computation.1 | async-start | bytes 3538944 | tf_op jit(solution)/shard_map/all_to_all | solution.py:174
  388.9 6.9 copy-start.48
  413.8 74.7 %all-to-all-start.3 = ((bf16[8,144,768]{2,1,0:T(8,128)(2,1)}), bf16[8,144,768]{2,1,0:T(8,128)(2,1)}, u32[]{:S(2)}, u32[]{:S(2)}) async-start(bf16[8,144,768]{2,1,0:T(8,128)(2,1)} %bitcast.276), calls=%async_computation.3 | async-start | bytes 3538944 | tf_op jit(solution)/shard_map/all_to_all | solution.py:232
  418.1 317.8 %reduce-scatter.4.cloned.1.call-start = ((), (), s32[]{:S(2)}) async-start(), calls=%async_computation.8 | async-start | bytes 3932160 | tf_op jit(solution)/shard_map/reduce_scatter | solution.py:307
  437.4 45.5 %copy-start.21 = (f32[768]{0:T(1024)S(1)}, f32[768]{0:T(1024)}, u32[]{:S(2)}) copy-start(f32[768]{0:T(1024)} %copy-done.20) | copy-start | bytes 9220
  437.4 47.8 %copy-start.19 = (f32[768,2,2]{0,2,1:T(2,128)S(1)}, f32[768,2,2]{0,2,1:T(2,128)}, u32[]{:S(2)}) copy-start(f32[768,2,2]{0,2,1:T(2,128)} %copy-done.18) | copy-start | bytes 36868
  488.5 13.2 %copy-start.26 = (f32[768]{0:T(1024)S(1)}, f32[768]{0:T(1024)}, u32[]{:S(2)}) copy-start(f32[768]{0:T(1024)} %copy-done.25) | copy-start | bytes 9220
  501.7 7.1 copy-start.5
  501.8 7.1 copy-start.6
  501.8 7.0 copy-start.10
  501.8 7.0 copy-start.31
  501.8 7.0 copy-start.38
  690.4 249.8 %all-reduce.8.cloned.1.call-start = ((), (), s32[]{:S(2)}) async-start(), calls=%async_computation.11 | async-start | bytes 18874368 | tf_op jit(solution)/shard_map/psum | solution.py:317
  693.5 42.4 %copy-start.37 = (f32[768]{0:T(1024)S(1)}, f32[768]{0:T(1024)}, u32[]{:S(2)}) copy-start(f32[768]{0:T(1024)} %copy-done.36) | copy-start | bytes 9220
  744.4 242.8 %reduce-scatter.8.cloned.1.call-start = ((), (), s32[]{:S(2)}) async-start(), calls=%async_computation.10 | async-start | bytes 3932160 | tf_op jit(solution)/shard_map/reduce_scatter | solution.py:244
  753.5 307.7 %reduce-scatter.6.cloned.1.call-start = ((), (), s32[]{:S(2)}) async-start(), calls=%async_computation.9 | async-start | bytes 7864320 | tf_op jit(solution)/shard_map/reduce_scatter | solution.py:241
  771.3 482.5 %all-reduce.10.cloned.1.call-start = ((), (), s32[]{:S(2)}) async-start(), calls=%async_computation.12 | async-start | bytes 18874368 | tf_op jit(solution)/shard_map/psum | solution.py:316
  989.8 6.9 copy-start.29
  989.8 56.1 %copy-start.35 = (f32[768]{0:T(1024)S(1)}, f32[768]{0:T(1024)}, u32[]{:S(2)}) copy-start(f32[768]{0:T(1024)} %get-tuple-element.484) | copy-start | bytes 9220
  1253.8 6.6 copy-start.14
  (72 other events, 189.9 us)
Sparse Core Ops, SparseCore 0:
  17.3 46.6 all-gather.1
  690.6 45.2 reduce-scatter.3
  744.6 195.6 all-reduce.7
  943.1 44.0 reduce-scatter.7
  990.0 71.0 reduce-scatter.5
  1064.7 189.0 all-reduce.9
